TPU v7x, 32 devices: a whole 2x2x4 slice. The times are simulated.
32 devices in a mesh: xy: 16 (over z, y, core), gz: 2 (over x).
Axes of the slice: x: 2, y: 2, z: 4, core: 2. Of those that a mesh axis runs over, the one named last changes fastest.
Arguments:
- hidden_features: bfloat16 [16, 16, 16, 512], P('gz', None, 'xy'), may hold values from -6 to 6
- scaling_factors_prenormal: float32 [512], replicated, may hold values from 0.1 to 1.9
- attention_input_matrices: bfloat16 [3, 512, 1536], P(None, 'xy'), may hold values from -1 to 1
- final_projection_matrices: bfloat16 [3, 512, 512], P(None, 'xy'), may hold values from -0.25 to 0.25
- score_scaling: float32 [3, 8], replicated, may hold values from 0 to 40
- filled_pillar_positions: int32 [16, 16], P('xy'), may hold values from 0 to 15, as said below
- filled_pillar_totals: int32 [16], P('xy'), may hold values from 4 to 16, as said below
Outputs:
- block_out: bfloat16 [16, 16, 16, 512], P('gz', None, 'xy')
Inputs may be any that keep to these rules, and one draw needn't show every extreme that they name: Row t of filled_pillar_positions is a permutation of 0 to 15; an entry c names the column x = c, y = t. `filled_pillar_totals`: some tile has all of its 16 columns occupied.
All inputs are finite; a program needn't handle non-finite values.
Results may differ from a plain program's by a relative error of at most 0.012.
Values may be sent and summed in bfloat16 or wider, within the bound.
No kernel may reach another device: no remote copies, remote signals or barrier semaphores. Data moves between devices by JAX's collectives and lax.ppermute only.
A program may use at most 64 MiB of HBM per device.

v0:
```python
import math
import jax
import jax.numpy as jnp
from jax import lax
from jax.sharding import PartitionSpec as P

EPSILON = 1e-06


def rms_scale(vector_rows):
    return vector_rows * lax.rsqrt(
        jnp.mean(vector_rows * vector_rows, axis=-1, keepdims=True) + EPSILON
    )


def project_qkv(tokens_in, w_project, attention_parts_number):
    projected = jnp.dot(tokens_in, w_project, preferred_element_type=jnp.float32)
    outer_shape = projected.shape[:-1]
    channels = w_project.shape[0]
    split_rows = projected.reshape(
        outer_shape + (3, attention_parts_number, channels // attention_parts_number)
    )
    queries = (
        rms_scale(split_rows[..., 0, :, :]).reshape(outer_shape + (channels,)).astype(jnp.bfloat16)
    )
    key_rows = (
        rms_scale(split_rows[..., 1, :, :]).reshape(outer_shape + (channels,)).astype(jnp.bfloat16)
    )
    values = split_rows[..., 2, :, :].reshape(outer_shape + (channels,)).astype(jnp.bfloat16)
    return (queries, key_rows, values)


def softmax_over_fibers(queries, key_rows, values, temper_row):
    attention_parts_number = temper_row.shape[0]
    outer_size, query_len, inner_size, channels = queries.shape
    key_len = key_rows.shape[1]
    head_dim = channels // attention_parts_number
    query_heads = queries.reshape(
        outer_size, query_len, inner_size, attention_parts_number, head_dim
    )
    key_heads = key_rows.reshape(outer_size, key_len, inner_size, attention_parts_number, head_dim)
    value_heads = values.reshape(outer_size, key_len, inner_size, attention_parts_number, head_dim)
    scores = jnp.einsum(
        "anbhd,ambhd->abhnm", query_heads, key_heads, preferred_element_type=jnp.float32
    )
    scores = scores * (temper_row / math.sqrt(head_dim))[None, None, :, None, None]
    weights = jax.nn.softmax(scores, axis=-1).astype(jnp.bfloat16)
    mixture = jnp.einsum(
        "abhnm,ambhd->anbhd", weights, value_heads, preferred_element_type=jnp.float32
    )
    return mixture.astype(jnp.bfloat16).reshape(outer_size, query_len, inner_size, channels)


def out_project(mixture, w_back):
    return jnp.dot(mixture, w_back, preferred_element_type=jnp.float32).astype(jnp.bfloat16)


def shards(
    hidden_features,
    scaling_factors_prenormal,
    attention_input_matrices,
    final_projection_matrices,
    score_scaling,
    filled_pillar_positions,
    filled_pillar_totals,
):
    full_qkv, full_out = (
        lax.all_gather(attention_input_matrices, "xy", axis=1, tiled=True),
        lax.all_gather(final_projection_matrices, "xy", axis=1, tiled=True),
    )
    attention_parts_number = score_scaling.shape[1]
    x_local, z_cells, y_rows, channels = hidden_features.shape
    normed = (rms_scale(hidden_features.astype(jnp.float32)) * scaling_factors_prenormal).astype(
        jnp.bfloat16
    )
    y_lines = normed.reshape(x_local * z_cells, y_rows, channels)
    local_query, local_keys, local_values = project_qkv(
        y_lines, full_qkv[1], attention_parts_number
    )
    query_along_y, keys_along_y, values_along_y = (
        lax.all_to_all(local_query, "xy", split_axis=0, concat_axis=1, tiled=True),
        lax.all_to_all(local_keys, "xy", split_axis=0, concat_axis=1, tiled=True),
        lax.all_to_all(local_values, "xy", split_axis=0, concat_axis=1, tiled=True),
    )
    y_mix = softmax_over_fibers(
        query_along_y[:, :, None, :],
        keys_along_y[:, :, None, :],
        values_along_y[:, :, None, :],
        score_scaling[1],
    )[:, :, 0, :]
    second_direction_answer = lax.all_to_all(
        out_project(y_mix, full_out[1]), "xy", split_axis=1, concat_axis=0, tiled=True
    ).reshape(hidden_features.shape)
    pieces = project_qkv(
        lax.all_to_all(normed, "gz", split_axis=1, concat_axis=0, tiled=True),
        full_qkv[0],
        attention_parts_number,
    )
    full_len, slab_part, items, _ = pieces[0].shape
    shaped = (1, full_len, slab_part * items, channels)
    x_mix = softmax_over_fibers(
        pieces[0].reshape(shaped),
        pieces[1].reshape(shaped),
        pieces[2].reshape(shaped),
        score_scaling[0],
    )
    result_rows = out_project(x_mix, full_out[0]).reshape(full_len, slab_part, items, channels)
    first_direction_answer = lax.all_to_all(
        result_rows, "gz", split_axis=0, concat_axis=1, tiled=True
    )
    cols_here = x_local * y_rows
    total_cols = filled_pillar_positions.shape[1]
    my_cols = lax.axis_index("gz") * cols_here + jnp.arange(cols_here, dtype=jnp.int32)
    live_rank = jnp.arange(total_cols, dtype=jnp.int32) < filled_pillar_totals[0]
    matches = filled_pillar_positions[0][None, :] == my_cols[:, None]
    live = jnp.any(jnp.logical_and(matches, live_rank[None, :]), axis=1)
    vertical_asking_terms, vertical_matching_terms, vertical_content_terms = project_qkv(
        normed, full_qkv[2], attention_parts_number
    )
    vertical_blended = softmax_over_fibers(
        vertical_asking_terms, vertical_matching_terms, vertical_content_terms, score_scaling[2]
    )
    z_full = out_project(vertical_blended, full_out[2])
    live_grid = live.reshape(x_local, 1, y_rows, 1)
    vertical_answer = jnp.where(live_grid, z_full, jnp.zeros_like(z_full))
    summed = (
        hidden_features.astype(jnp.float32)
        + first_direction_answer.astype(jnp.float32)
        + second_direction_answer.astype(jnp.float32)
    )
    summed = summed + vertical_answer.astype(jnp.float32)
    return summed.astype(jnp.bfloat16)


def solution(mesh):
    in_specs = (
        P("gz", None, "xy", None),
        P(),
        P(None, "xy", None),
        P(None, "xy", None),
        P(),
        P("xy", None),
        P("xy"),
    )
    out_specs = P("gz", None, "xy", None)
    return jax.shard_map(shards, mesh=mesh, in_specs=in_specs, out_specs=out_specs, check_vma=False)
```

profile of v0, /device:TPU:0, one launch (start us, length us, event | category | flops | bytes accessed | tf_op | source)
XLA Modules:
  0.0 148.3 jit_solution(13666185661406171766)
XLA Ops:
  7.3 1.0 fusion.23
  8.3 1.0 fusion.25
  10.0 4.2 %all-to-all-start = ((bf16[8,16,1,512]{3,0,2,1:T(8,128)(2,1)}), bf16[8,16,1,512]{3,0,2,1:T(8,128)(2,1)S(1)}, u32[]{:S(2)}, u32[]{:S(2)}) async-start(bf16[8,16,1,512]{3,0,2,1:T(8,128)(2,1)} %copy.102), calls=%async_computation | async-start | bytes 262144 | tf_op jit(solution)/shard_map/all_to_all | solution.py:95
  15.0 0.8 multiply_bitcast_fusion.2
  16.5 0.8 and_reduce_fusion
  17.3 1.5 %all-to-all-done = bf16[8,16,1,512]{3,0,2,1:T(8,128)(2,1)S(1)} async-done(((bf16[8,16,1,512]{3,0,2,1:T(8,128)(2,1)}), bf16[8,16,1,512]{3,0,2,1:T(8,128)(2,1)S(1)}, u32[]{:S(2)}, u32[]{:S(2)}) %all-to-all-start) | async-done | bytes 131104 | tf_op jit(solution)/shard_map/all_to_all | solution.py:95
  19.5 46.0 %all-gather.3.cloned.1.call-done = bf16[3,512,1536]{2,1,0:T(8,128)(2,1)} async-done(((bf16[3,32,1536]{2,1,0:T(8,128)(2,1)}), bf16[3,512,1536]{2,1,0:T(8,128)(2,1)}) %all-gather.3.cloned.1.call-update) | async-done | bytes 4718608 | tf_op jit(solution)/shard_map/all_gather | solution.py:68
  65.5 4.4 %slice_bitcast_fusion.2 = (bf16[1536,512]{0,1:T(8,128)(2,1)}, bf16[1536,512]{0,1:T(8,128)(2,1)S(1)}, bf16[1536,512]{0,1:T(8,128)(2,1)}) fusion(bf16[3,512,1536]{2,1,0:T(8,128)(2,1)} %all-gather.3.cloned.1.call-done), kind=kLoop, calls=%fused_computation.5 | loop fusion | bytes 9437184 | tf_op jit(solution)/shard_map/dot_general | solution.py:17
  69.9 1.7 %copy.104 = bf16[1536,512]{1,0:T(8,128)(2,1)S(1)} copy(bf16[1536,512]{0,1:T(8,128)(2,1)} %get-tuple-element.11) | data formatting | bytes 3145728 | tf_op jit(solution)/shard_map/dot_general | solution.py:17
  71.6 2.6 %copy.112 = bf16[1536,512]{1,0:T(8,128)(2,1)} copy(bf16[1536,512]{0,1:T(8,128)(2,1)} %get-tuple-element.13) | data formatting | bytes 3145728 | tf_op jit(solution)/shard_map/dot_general | solution.py:17
  74.3 2.0 %convolution_bitcast_fusion.2 = f32[128,1,3,8,64]{0,4,3,2,1:T(8,128)S(1)} fusion(bf16[128,512,1,1]{1,0,3,2:T(8,128)(2,1)S(1)} %bitcast.200, bf16[3,8,64,512]{3,2,1,0:T(8,128)(2,1)} %bitcast.199), kind=kOutput, calls=%fused_computation.8 | convolution fusion | flops 201326592 | bytes 2490368 | tf_op jit(solution)/shard_map/dot_general | solution.py:17
  76.3 0.9 copy-done
  77.8 1.2 reduce.26
  79.0 1.0 copy.180
  80.8 3.5 %all-to-all-start.3 = ((bf16[16,2,2048]{2,1,0:T(2,128)(2,1)}), bf16[16,2,2048]{2,1,0:T(2,128)(2,1)S(1)}, u32[]{:S(2)}, u32[]{:S(2)}) async-start(bf16[16,2,2048]{2,1,0:T(2,128)(2,1)} %reshape.552), calls=%async_computation.3 | async-start | bytes 262144 | tf_op jit(solution)/shard_map/all_to_all | solution.py:81
  84.3 1.8 %convolution_bitcast_fusion.1 = f32[16,8,1,3,8,64]{5,1,4,3,0,2:T(8,128)S(1)} fusion(bf16[16,8,512,1,1]{2,1,4,3,0:T(8,128)(2,1)} %bitcast.207, bf16[3,8,64,512,1]{3,2,1,0,4:T(8,128)(2,1)S(1)} %bitcast.197), kind=kOutput, calls=%fused_computation.7 | convolution fusion | flops 201326592 | bytes 2490368 | tf_op jit(solution)/shard_map/dot_general | solution.py:17
  87.7 1.0 fusion.9
  90.8 0.9 convolution_bitcast_fusion
  92.2 5.8 %all-to-all-start.4 = ((bf16[16,2,2048]{2,1,0:T(2,128)(2,1)}), bf16[16,2,2048]{2,1,0:T(2,128)(2,1)S(1)}, u32[]{:S(2)}, u32[]{:S(2)}) async-start(bf16[16,2,2048]{2,1,0:T(2,128)(2,1)} %reshape.550), calls=%async_computation.4 | async-start | bytes 262144 | tf_op jit(solution)/shard_map/all_to_all | solution.py:82
  98.3 1.0 slice.122
  101.0 5.2 %all-to-all-done.4 = bf16[16,2,2048]{2,1,0:T(2,128)(2,1)S(1)} async-done(((bf16[16,2,2048]{2,1,0:T(2,128)(2,1)}), bf16[16,2,2048]{2,1,0:T(2,128)(2,1)S(1)}, u32[]{:S(2)}, u32[]{:S(2)}) %all-to-all-start.4) | async-done | bytes 131104 | tf_op jit(solution)/shard_map/all_to_all | solution.py:82
  106.2 3.5 %all-to-all-start.2 = ((bf16[16,2,2048]{2,1,0:T(2,128)(2,1)}), bf16[16,2,2048]{2,1,0:T(2,128)(2,1)S(1)}, u32[]{:S(2)}, u32[]{:S(2)}) async-start(bf16[16,2,2048]{2,1,0:T(2,128)(2,1)} %reshape.554), calls=%async_computation.2 | async-start | bytes 262144 | tf_op jit(solution)/shard_map/all_to_all | solution.py:83
  109.8 2.0 %fusion.54 = (f32[8,8,16]{2,1,0:T(8,128)}, f32[8,8,16,16]{2,3,1,0:T(8,128)}) fusion(f32[8,16,1,3,8,64]{5,1,4,3,0,2:T(8,128)S(1)} %convolution_bitcast_fusion, f32[8]{0:T(128)S(1)} %get-tuple-element.19, f32[8,16,8]{1,2,0:T(8,128)S(1)} %get-tuple-element.27, f32[8,16,8]{1,2,0:T(8,128)S(1)} %get-tuple-element.28), kind=kOutput, calls=%fused_computation.99 | convolution fusion | flops 2408463 | bytes 1184256 | tf_op jit(solution)/shard_map/sub | solution.py:47
  112.4 5.2 %all-to-all-done.2 = bf16[16,2,2048]{2,1,0:T(2,128)(2,1)S(1)} async-done(((bf16[16,2,2048]{2,1,0:T(2,128)(2,1)}), bf16[16,2,2048]{2,1,0:T(2,128)(2,1)S(1)}, u32[]{:S(2)}, u32[]{:S(2)}) %all-to-all-start.2) | async-done | bytes 131104 | tf_op jit(solution)/shard_map/all_to_all | solution.py:83
  119.1 1.3 convolution_convert_fusion.4
  121.2 3.6 %all-to-all-start.5 = ((bf16[8,16,512]{2,0,1:T(8,128)(2,1)}), bf16[8,16,512]{2,0,1:T(8,128)(2,1)S(1)}, u32[]{:S(2)}, u32[]{:S(2)}) async-start(bf16[8,16,512]{2,0,1:T(8,128)(2,1)} %copy.124), calls=%async_computation.5 | async-start | bytes 262144 | tf_op jit(solution)/shard_map/all_to_all | solution.py:91
  124.8 1.3 fusion.11
  126.4 0.9 fusion.12
  127.3 5.3 %all-to-all-done.5 = bf16[8,16,512]{2,0,1:T(8,128)(2,1)S(1)} async-done(((bf16[8,16,512]{2,0,1:T(8,128)(2,1)}), bf16[8,16,512]{2,0,1:T(8,128)(2,1)S(1)}, u32[]{:S(2)}, u32[]{:S(2)}) %all-to-all-start.5) | async-done | bytes 131104 | tf_op jit(solution)/shard_map/all_to_all | solution.py:91
  132.7 3.4 %all-to-all-start.1 = ((bf16[16,8,1,512]{3,1,2,0:T(8,128)(2,1)}), bf16[16,8,1,512]{3,1,2,0:T(8,128)(2,1)S(1)}, u32[]{:S(2)}, u32[]{:S(2)}) async-start(bf16[16,8,1,512]{3,1,2,0:T(8,128)(2,1)} %fusion.12), calls=%async_computation.1 | async-start | bytes 262144 | tf_op jit(solution)/shard_map/all_to_all | solution.py:108
  136.1 4.4 %all-to-all-done.1 = bf16[16,8,1,512]{3,1,2,0:T(8,128)(2,1)S(1)} async-done(((bf16[16,8,1,512]{3,1,2,0:T(8,128)(2,1)}), bf16[16,8,1,512]{3,1,2,0:T(8,128)(2,1)S(1)}, u32[]{:S(2)}, u32[]{:S(2)}) %all-to-all-start.1) | async-done | bytes 131104 | tf_op jit(solution)/shard_map/all_to_all | solution.py:108
  140.5 0.9 fusion.18
  (61 shorter events, 13.5 us)
Async XLA Ops:
  6.5 59.0 %all-gather.3.cloned.1.call-start = ((), (), s32[]{:S(2)}) async-start(), calls=%async_computation.6 | async-start | bytes 5013504 | tf_op jit(solution)/shard_map/all_gather | solution.py:68
  10.0 8.8 %all-to-all-start = ((bf16[8,16,1,512]{3,0,2,1:T(8,128)(2,1)}), bf16[8,16,1,512]{3,0,2,1:T(8,128)(2,1)S(1)}, u32[]{:S(2)}, u32[]{:S(2)}) async-start(bf16[8,16,1,512]{3,0,2,1:T(8,128)(2,1)} %copy.102), calls=%async_computation | async-start | bytes 262144 | tf_op jit(solution)/shard_map/all_to_all | solution.py:95
  14.3 104.9 %all-gather.5.cloned.1.call-start = ((), (), s32[]{:S(2)}) async-start(), calls=%async_computation.7 | async-start | bytes 1671168 | tf_op jit(solution)/shard_map/all_gather | solution.py:69
  76.2 0.9 copy-start
  80.8 11.4 %all-to-all-start.3 = ((bf16[16,2,2048]{2,1,0:T(2,128)(2,1)}), bf16[16,2,2048]{2,1,0:T(2,128)(2,1)S(1)}, u32[]{:S(2)}, u32[]{:S(2)}) async-start(bf16[16,2,2048]{2,1,0:T(2,128)(2,1)} %reshape.552), calls=%async_computation.3 | async-start | bytes 262144 | tf_op jit(solution)/shard_map/all_to_all | solution.py:81
  91.7 7.5 %copy-start.3 = (bf16[1,16,8,8,64]{4,1,3,2,0:T(8,128)(2,1)S(1)}, bf16[1,16,8,8,64]{4,1,3,2,0:T(8,128)(2,1)}, u32[]{:S(2)}) copy-start(bf16[1,16,8,8,64]{4,1,3,2,0:T(8,128)(2,1)} %fusion.9) | copy-start | bytes 393220
  92.2 14.1 %all-to-all-start.4 = ((bf16[16,2,2048]{2,1,0:T(2,128)(2,1)}), bf16[16,2,2048]{2,1,0:T(2,128)(2,1)S(1)}, u32[]{:S(2)}, u32[]{:S(2)}) async-start(bf16[16,2,2048]{2,1,0:T(2,128)(2,1)} %reshape.550), calls=%async_computation.4 | async-start | bytes 262144 | tf_op jit(solution)/shard_map/all_to_all | solution.py:82
  106.2 11.4 %all-to-all-start.2 = ((bf16[16,2,2048]{2,1,0:T(2,128)(2,1)}), bf16[16,2,2048]{2,1,0:T(2,128)(2,1)S(1)}, u32[]{:S(2)}, u32[]{:S(2)}) async-start(bf16[16,2,2048]{2,1,0:T(2,128)(2,1)} %reshape.554), calls=%async_computation.2 | async-start | bytes 262144 | tf_op jit(solution)/shard_map/all_to_all | solution.py:83
  118.8 6.0 %copy-start.4 = (f32[8,8,16]{2,1,0:T(8,128)S(1)}, f32[8,8,16]{2,1,0:T(8,128)}, u32[]{:S(2)}) copy-start(f32[8,8,16]{2,1,0:T(8,128)} %get-tuple-element.21) | copy-start | bytes 12292
  121.1 5.3 %copy-start.2 = (bf16[3,512,512]{2,1,0:T(8,128)(2,1)S(1)}, bf16[3,512,512]{2,1,0:T(8,128)(2,1)}, u32[]{:S(2)}) copy-start(bf16[3,512,512]{2,1,0:T(8,128)(2,1)} %all-gather.5.cloned.1.call-done) | copy-start | bytes 4718596
  121.2 11.5 %all-to-all-start.5 = ((bf16[8,16,512]{2,0,1:T(8,128)(2,1)}), bf16[8,16,512]{2,0,1:T(8,128)(2,1)S(1)}, u32[]{:S(2)}, u32[]{:S(2)}) async-start(bf16[8,16,512]{2,0,1:T(8,128)(2,1)} %copy.124), calls=%async_computation.5 | async-start | bytes 262144 | tf_op jit(solution)/shard_map/all_to_all | solution.py:91
  126.1 14.4 %copy-start.1 = (bf16[8,16,1,512]{3,1,2,0:T(8,128)(2,1)S(1)}, bf16[8,16,1,512]{3,1,2,0:T(8,128)(2,1)}, u32[]{:S(2)}) copy-start(bf16[8,16,1,512]{3,1,2,0:T(8,128)(2,1)} %param.7) | copy-start | bytes 393220
  132.7 7.8 %all-to-all-start.1 = ((bf16[16,8,1,512]{3,1,2,0:T(8,128)(2,1)}), bf16[16,8,1,512]{3,1,2,0:T(8,128)(2,1)S(1)}, u32[]{:S(2)}, u32[]{:S(2)}) async-start(bf16[16,8,1,512]{3,1,2,0:T(8,128)(2,1)} %fusion.12), calls=%async_computation.1 | async-start | bytes 262144 | tf_op jit(solution)/shard_map/all_to_all | solution.py:108
Sparse Core Ops, SparseCore 0:
  9.6 55.8 all-gather.2
  67.7 39.1 all-gather.4
where the time goes:
time: 149 us; the launch traced here: 148 us
  waiting for transfers between devices  69.6 us (47%)
  starting transfers between devices  24.1 us (16%)
  local copies, waits for them, and re-layouts  19.2 us (13%)
  between operations  14.4 us (10%)
  matrix products  13.7 us (9%)
  other arithmetic  7.31 us (5%)
    all_gather x1, waiting for transfers between devices, shards(): lax.all_gather(attention_input_matrices, 'xy', axis=1, tiled=True)  46 us
    dot_general x4, local copies, waits for them, and re-layouts, project_qkv(): jnp.dot(tokens_in, w_project, preferred_element_type=jnp.float32)  9.41 us
    all_to_all x1, starting transfers between devices, shards(): lax.all_to_all(local_keys, 'xy', split_axis=0, concat_axis=1, tiled=True)  5.78 us
    all_to_all x1, waiting for transfers between devices, shards(): lax.all_to_all(out_project(y_mix, full_out[1]), 'xy', split_axis=1, conca...  5.35 us
    all_to_all x1, waiting for transfers between devices, shards(): lax.all_to_all(local_keys, 'xy', split_axis=0, concat_axis=1, tiled=True)  5.24 us
    all_to_all x1, waiting for transfers between devices, shards(): lax.all_to_all(local_values, 'xy', split_axis=0, concat_axis=1, tiled=True)  5.21 us
    dot_general x3, matrix products, project_qkv(): jnp.dot(tokens_in, w_project, preferred_element_type=jnp.float32)  4.68 us
    unnamed x22, local copies, waits for them, and re-layouts  4.68 us
  transfers between devices with their start and end apart: 8, of which 7 were waited for; matrix products, arithmetic and copies ran while one was open for 25% of the time, Pallas kernels for 0%

commit v1 on v0

--- a/solution.py
+++ b/solution.py
@@ -79,7 +79,12 @@
     )
     query_along_y, keys_along_y, values_along_y = (
         lax.all_to_all(local_query, "xy", split_axis=0, concat_axis=1, tiled=True),
-        lax.all_to_all(local_keys, "xy", split_axis=0, concat_axis=1, tiled=True),
+        jnp.concatenate(
+            lax.all_to_all(
+                jnp.stack(jnp.split(local_keys, lax.axis_size("xy"), axis=0)), "xy", 0, 0
+            ),
+            axis=1,
+        ),
         lax.all_to_all(local_values, "xy", split_axis=0, concat_axis=1, tiled=True),
     )
     y_mix = softmax_over_fibers(

time: 149 us -> 191 us (1.28)
  local copies, waits for them, and re-layouts: 19.2 us -> 60.6 us
    another operation x5 -> x21, local copies, waits for them, and re-layouts: 0.97 us -> 24.8 us  [the longest x16 22.9 us: shards(): jnp.stack(jnp.split(local_keys, lax.axis_size('xy'), axis=0))]
    unnamed x22 -> x39, local copies, waits for them, and re-layouts: 4.68 us -> 20.7 us
    all_to_all x1, waiting for transfers between devices: 5.24 us -> 0.01 us  [shards(): lax.all_to_all(jnp.stack(jnp.split(local_keys, lax.axis_size('xy'), axis=...]
    all_to_all x1, waiting for transfers between devices: 0.39 us -> 4.77 us  [shards(): lax.all_to_all(local_query, 'xy', split_axis=0, concat_axis=1, tiled=True)]
    split x0 -> x2, local copies, waits for them, and re-layouts: none -> 2.81 us  [shards(): jnp.split(local_keys, lax.axis_size('xy'), axis=0)]
    all_to_all x1, starting transfers between devices: 3.51 us -> 6.05 us  [shards(): lax.all_to_all(local_query, 'xy', split_axis=0, concat_axis=1, tiled=True)]
  transfers between devices with their start and end apart: 8 -> 8, of which waited for: 7 -> 6; matrix products, arithmetic and copies ran while one was open for 25% -> 41% of each run, Pallas kernels for 0% -> 0%
where the time goes in v1:
time: 191 us; the launch traced here: 189 us
  waiting for transfers between devices  68.1 us (36%)
  local copies, waits for them, and re-layouts  60.6 us (32%)
  starting transfers between devices  25 us (13%)
  between operations  14.5 us (8%)
  matrix products  13.6 us (7%)
  other arithmetic  7.36 us (4%)
    all_gather x1, waiting for transfers between devices, shards(): lax.all_gather(attention_input_matrices, 'xy', axis=1, tiled=True)  46.7 us
    another operation x16, local copies, waits for them, and re-layouts, shards(): jnp.stack(jnp.split(local_keys, lax.axis_size('xy'), axis=0))  22.9 us
    unnamed x39, local copies, waits for them, and re-layouts  20.7 us
    dot_general x4, local copies, waits for them, and re-layouts, project_qkv(): jnp.dot(tokens_in, w_project, preferred_element_type=jnp.float32)  8.8 us
    all_to_all x1, starting transfers between devices, shards(): lax.all_to_all(local_query, 'xy', split_axis=0, concat_axis=1, tiled=True)  6.05 us
    all_to_all x1, waiting for transfers between devices, shards(): lax.all_to_all(out_project(y_mix, full_out[1]), 'xy', split_axis=1, conca...  5.35 us
    dot_general x3, matrix products, project_qkv(): jnp.dot(tokens_in, w_project, preferred_element_type=jnp.float32)  5.2 us
    all_to_all x1, waiting for transfers between devices, shards(): lax.all_to_all(local_values, 'xy', split_axis=0, concat_axis=1, tiled=True)  5.04 us
  transfers between devices with their start and end apart: 8, of which 6 were waited for; matrix products, arithmetic and copies ran while one was open for 41% of the time, Pallas kernels for 0%

profile of v1, /device:TPU:0, one launch (start us, length us, event | category | flops | bytes accessed | tf_op | source)
XLA Modules:
  0.0 189.1 jit_solution(14396144874076290056)
XLA Ops:
  10.0 4.2 %all-to-all-start = ((bf16[8,16,1,512]{3,0,2,1:T(8,128)(2,1)}), bf16[8,16,1,512]{3,0,2,1:T(8,128)(2,1)S(1)}, u32[]{:S(2)}, u32[]{:S(2)}) async-start(bf16[8,16,1,512]{3,0,2,1:T(8,128)(2,1)} %copy.132), calls=%async_computation | async-start | bytes 262144 | tf_op jit(solution)/shard_map/all_to_all | solution.py:100
  15.0 1.4 multiply_bitcast_fusion.2
  17.0 1.4 and_reduce_fusion
  18.9 46.7 %all-gather.3.cloned.1.call-done = bf16[3,512,1536]{2,1,0:T(8,128)(2,1)} async-done(((bf16[3,32,1536]{2,1,0:T(8,128)(2,1)}), bf16[3,512,1536]{2,1,0:T(8,128)(2,1)}) %all-gather.3.cloned.1.call-update) | async-done | bytes 4718608 | tf_op jit(solution)/shard_map/all_gather | solution.py:68
  65.5 3.9 %slice_bitcast_fusion.2 = (bf16[1536,512]{0,1:T(8,128)(2,1)S(1)}, bf16[1536,512]{0,1:T(8,128)(2,1)S(1)}, bf16[1536,512]{0,1:T(8,128)(2,1)}) fusion(bf16[3,512,1536]{2,1,0:T(8,128)(2,1)} %all-gather.3.cloned.1.call-done), kind=kLoop, calls=%fused_computation.5 | loop fusion | bytes 9437184 | tf_op jit(solution)/shard_map/dot_general | solution.py:17
  69.4 2.6 %copy.142 = bf16[1536,512]{1,0:T(8,128)(2,1)} copy(bf16[1536,512]{0,1:T(8,128)(2,1)} %get-tuple-element.13) | data formatting | bytes 3145728 | tf_op jit(solution)/shard_map/dot_general | solution.py:17
  72.0 2.0 %convolution_bitcast_fusion.2 = f32[128,1,3,8,64]{0,4,3,2,1:T(8,128)S(1)} fusion(bf16[128,512,1,1]{1,0,3,2:T(8,128)(2,1)S(1)} %bitcast.228, bf16[3,8,64,512]{3,2,1,0:T(8,128)(2,1)} %bitcast.227), kind=kOutput, calls=%fused_computation.8 | convolution fusion | flops 201326592 | bytes 2490368 | tf_op jit(solution)/shard_map/dot_general | solution.py:17
  74.9 1.8 fusion.54
  78.3 1.6 copy.149
  79.9 1.6 copy.150
  81.5 1.6 copy.151
  83.1 1.6 copy.152
  84.6 1.6 copy.153
  86.2 1.6 copy.154
  87.8 1.6 copy.155
  89.3 1.6 copy.156
  90.9 1.6 copy.157
  92.5 1.6 copy.158
  94.0 1.6 copy.159
  95.6 1.6 copy.160
  97.2 1.6 copy.161
  118.7 4.2 %all-to-all-start.4 = ((bf16[16,8,1,512]{3,1,2,0:T(8,128)(2,1)}), bf16[16,8,1,512]{3,1,2,0:T(8,128)(2,1)}, u32[]{:S(2)}, u32[]{:S(2)}) async-start(bf16[16,8,1,512]{3,1,2,0:T(8,128)(2,1)} %constant_dynamic-update-slice_fusion), calls=%async_computation.4 | async-start | bytes 262144 | tf_op jit(solution)/shard_map/all_to_all | solution.py:83
  122.8 1.6 copy.134
  124.4 2.3 %convolution_bitcast_fusion.1 = f32[16,8,1,3,8,64]{5,1,4,3,0,2:T(8,128)S(1)} fusion(bf16[16,8,512,1,1]{2,1,4,3,0:T(8,128)(2,1)S(1)} %bitcast.234, bf16[3,8,64,512,1]{3,2,1,0,4:T(8,128)(2,1)} %bitcast.225), kind=kOutput, calls=%fused_computation.7 | convolution fusion | flops 201326592 | bytes 2490368 | tf_op jit(solution)/shard_map/dot_general | solution.py:17
  133.1 6.0 %all-to-all-start.3 = ((bf16[16,2,2048]{2,1,0:T(2,128)(2,1)}), bf16[16,2,2048]{2,1,0:T(2,128)(2,1)S(1)}, u32[]{:S(2)}, u32[]{:S(2)}) async-start(bf16[16,2,2048]{2,1,0:T(2,128)(2,1)} %reshape.553), calls=%async_computation.3 | async-start | bytes 262144 | tf_op jit(solution)/shard_map/all_to_all | solution.py:81
  142.3 4.8 %all-to-all-done.3 = bf16[16,2,2048]{2,1,0:T(2,128)(2,1)S(1)} async-done(((bf16[16,2,2048]{2,1,0:T(2,128)(2,1)}), bf16[16,2,2048]{2,1,0:T(2,128)(2,1)S(1)}, u32[]{:S(2)}, u32[]{:S(2)}) %all-to-all-start.3) | async-done | bytes 131104 | tf_op jit(solution)/shard_map/all_to_all | solution.py:81
  147.1 3.5 %all-to-all-start.2 = ((bf16[16,2,2048]{2,1,0:T(2,128)(2,1)}), bf16[16,2,2048]{2,1,0:T(2,128)(2,1)S(1)}, u32[]{:S(2)}, u32[]{:S(2)}) async-start(bf16[16,2,2048]{2,1,0:T(2,128)(2,1)} %reshape.555), calls=%async_computation.2 | async-start | bytes 262144 | tf_op jit(solution)/shard_map/all_to_all | solution.py:88
  153.4 5.0 %all-to-all-done.2 = bf16[16,2,2048]{2,1,0:T(2,128)(2,1)S(1)} async-done(((bf16[16,2,2048]{2,1,0:T(2,128)(2,1)}), bf16[16,2,2048]{2,1,0:T(2,128)(2,1)S(1)}, u32[]{:S(2)}, u32[]{:S(2)}) %all-to-all-start.2) | async-done | bytes 131104 | tf_op jit(solution)/shard_map/all_to_all | solution.py:88
  162.0 3.6 %all-to-all-start.5 = ((bf16[8,16,512]{2,0,1:T(8,128)(2,1)}), bf16[8,16,512]{2,0,1:T(8,128)(2,1)S(1)}, u32[]{:S(2)}, u32[]{:S(2)}) async-start(bf16[8,16,512]{2,0,1:T(8,128)(2,1)} %copy.169), calls=%async_computation.5 | async-start | bytes 262144 | tf_op jit(solution)/shard_map/all_to_all | solution.py:96
  168.2 5.3 %all-to-all-done.5 = bf16[8,16,512]{2,0,1:T(8,128)(2,1)S(1)} async-done(((bf16[8,16,512]{2,0,1:T(8,128)(2,1)}), bf16[8,16,512]{2,0,1:T(8,128)(2,1)S(1)}, u32[]{:S(2)}, u32[]{:S(2)}) %all-to-all-start.5) | async-done | bytes 131104 | tf_op jit(solution)/shard_map/all_to_all | solution.py:96
  173.5 3.4 %all-to-all-start.1 = ((bf16[16,8,1,512]{3,1,2,0:T(8,128)(2,1)}), bf16[16,8,1,512]{3,1,2,0:T(8,128)(2,1)S(1)}, u32[]{:S(2)}, u32[]{:S(2)}) async-start(bf16[16,8,1,512]{3,1,2,0:T(8,128)(2,1)} %fusion.12), calls=%async_computation.1 | async-start | bytes 262144 | tf_op jit(solution)/shard_map/all_to_all | solution.py:113
  176.9 4.4 %all-to-all-done.1 = bf16[16,8,1,512]{3,1,2,0:T(8,128)(2,1)S(1)} async-done(((bf16[16,8,1,512]{3,1,2,0:T(8,128)(2,1)}), bf16[16,8,1,512]{3,1,2,0:T(8,128)(2,1)S(1)}, u32[]{:S(2)}, u32[]{:S(2)}) %all-to-all-start.1) | async-done | bytes 131104 | tf_op jit(solution)/shard_map/all_to_all | solution.py:113
  (95 shorter events, 46.0 us)
Async XLA Ops:
  6.5 59.0 %all-gather.3.cloned.1.call-start = ((), (), s32[]{:S(2)}) async-start(), calls=%async_computation.6 | async-start | bytes 5013504 | tf_op jit(solution)/shard_map/all_gather | solution.py:68
  10.0 8.8 %all-to-all-start = ((bf16[8,16,1,512]{3,0,2,1:T(8,128)(2,1)}), bf16[8,16,1,512]{3,0,2,1:T(8,128)(2,1)S(1)}, u32[]{:S(2)}, u32[]{:S(2)}) async-start(bf16[8,16,1,512]{3,0,2,1:T(8,128)(2,1)} %copy.132), calls=%async_computation | async-start | bytes 262144 | tf_op jit(solution)/shard_map/all_to_all | solution.py:100
  14.3 145.7 %all-gather.5.cloned.1.call-start = ((), (), s32[]{:S(2)}) async-start(), calls=%async_computation.7 | async-start | bytes 1671168 | tf_op jit(solution)/shard_map/all_gather | solution.py:69
  74.0 0.9 copy-start
  118.7 14.4 %all-to-all-start.4 = ((bf16[16,8,1,512]{3,1,2,0:T(8,128)(2,1)}), bf16[16,8,1,512]{3,1,2,0:T(8,128)(2,1)}, u32[]{:S(2)}, u32[]{:S(2)}) async-start(bf16[16,8,1,512]{3,1,2,0:T(8,128)(2,1)} %constant_dynamic-update-slice_fusion), calls=%async_computation.4 | async-start | bytes 262144 | tf_op jit(solution)/shard_map/all_to_all | solution.py:83
  126.7 0.8 copy-start.7
  133.1 8.9 %copy-start.3 = (bf16[1,16,8,8,64]{4,1,3,2,0:T(8,128)(2,1)S(1)}, bf16[1,16,8,8,64]{4,1,3,2,0:T(8,128)(2,1)}, u32[]{:S(2)}) copy-start(bf16[1,16,8,8,64]{4,1,3,2,0:T(8,128)(2,1)} %fusion.9) | copy-start | bytes 393220
  133.1 14.0 %all-to-all-start.3 = ((bf16[16,2,2048]{2,1,0:T(2,128)(2,1)}), bf16[16,2,2048]{2,1,0:T(2,128)(2,1)S(1)}, u32[]{:S(2)}, u32[]{:S(2)}) async-start(bf16[16,2,2048]{2,1,0:T(2,128)(2,1)} %reshape.553), calls=%async_computation.3 | async-start | bytes 262144 | tf_op jit(solution)/shard_map/all_to_all | solution.py:81
  139.2 11.4 %copy-start.6 = (f32[8]{0:T(128)S(1)}, f32[8]{0:T(128)}, u32[]{:S(2)}) copy-start(f32[8]{0:T(128)} %get-tuple-element.35) | copy-start | bytes 100
  147.1 11.4 %all-to-all-start.2 = ((bf16[16,2,2048]{2,1,0:T(2,128)(2,1)}), bf16[16,2,2048]{2,1,0:T(2,128)(2,1)S(1)}, u32[]{:S(2)}, u32[]{:S(2)}) async-start(bf16[16,2,2048]{2,1,0:T(2,128)(2,1)} %reshape.555), calls=%async_computation.2 | async-start | bytes 262144 | tf_op jit(solution)/shard_map/all_to_all | solution.py:88
  152.0 6.8 %copy-start.5 = (f32[8]{0:T(128)S(1)}, f32[8]{0:T(128)}, u32[]{:S(2)}) copy-start(f32[8]{0:T(128)} %get-tuple-element.36) | copy-start | bytes 100
  162.0 5.3 %copy-start.2 = (bf16[3,512,512]{2,1,0:T(8,128)(2,1)S(1)}, bf16[3,512,512]{2,1,0:T(8,128)(2,1)}, u32[]{:S(2)}) copy-start(bf16[3,512,512]{2,1,0:T(8,128)(2,1)} %all-gather.5.cloned.1.call-done) | copy-start | bytes 4718596
  162.0 11.5 %all-to-all-start.5 = ((bf16[8,16,512]{2,0,1:T(8,128)(2,1)}), bf16[8,16,512]{2,0,1:T(8,128)(2,1)S(1)}, u32[]{:S(2)}, u32[]{:S(2)}) async-start(bf16[8,16,512]{2,0,1:T(8,128)(2,1)} %copy.169), calls=%async_computation.5 | async-start | bytes 262144 | tf_op jit(solution)/shard_map/all_to_all | solution.py:96
  167.0 14.4 %copy-start.1 = (bf16[8,16,1,512]{3,1,2,0:T(8,128)(2,1)S(1)}, bf16[8,16,1,512]{3,1,2,0:T(8,128)(2,1)}, u32[]{:S(2)}) copy-start(bf16[8,16,1,512]{3,1,2,0:T(8,128)(2,1)} %param.7) | copy-start | bytes 393220
  167.0 14.4 %copy-start.4 = (pred[8]{0:T(512)(128)(4,1)S(1)}, pred[8]{0:T(512)(128)(4,1)}, u32[]{:S(2)}) copy-start(pred[8]{0:T(512)(128)(4,1)} %and_reduce_fusion) | copy-start | bytes 28
  173.5 7.8 %all-to-all-start.1 = ((bf16[16,8,1,512]{3,1,2,0:T(8,128)(2,1)}), bf16[16,8,1,512]{3,1,2,0:T(8,128)(2,1)S(1)}, u32[]{:S(2)}, u32[]{:S(2)}) async-start(bf16[16,8,1,512]{3,1,2,0:T(8,128)(2,1)} %fusion.12), calls=%async_computation.1 | async-start | bytes 262144 | tf_op jit(solution)/shard_map/all_to_all | solution.py:113
Sparse Core Ops, SparseCore 0:
  9.6 55.8 all-gather.2
  67.7 38.1 all-gather.4
